TPU v7x, 768 devices: a whole 4x8x12 slice. The times are simulated.
768 devices in a mesh: dp: 96 (over y, z_lo, core), tensor: 8 (over x, z_hi).
Axes of the slice: x: 4, y: 8, z: 12 (z_hi: 2, z_lo: 6; z = z_hi * 6 + z_lo), core: 2. Of those that a mesh axis runs over, the one named last changes fastest.
Arguments:
- tokens: bfloat16 [12288, 4096], P(('dp', 'tensor')), parts along dimension 0, may hold values from -6 to 6
- gate_act: bfloat16 [12288, 10240], P('dp', 'tensor'), parts along dimension 0, may hold values from -6 to 6
- up_act: bfloat16 [12288, 10240], P('dp', 'tensor'), parts along dimension 0, may hold values from -6 to 6
- down_weight: bfloat16 [10240, 4096], P('tensor'), may hold values from -0.0625 to 0.0625
- norm_gain: float32 [4096], replicated, may hold values from 0.25 to 1.75
Outputs:
- residual_out: bfloat16 [12288, 4096], P(('dp', 'tensor')), parts along dimension 0
- next_rows: bfloat16 [12288, 4096], P('dp'), parts along dimension 0
- next_scale: float32 [12288], P('dp'), parts along dimension 0
There are 96 independent parts, one for each index of `dp`. A program takes and returns all parts, laid end to end along the dimension named above; an argument that names none is the same for every part. Nothing has to cross between parts.
All inputs are finite; a program needn't handle non-finite values. Where the computation divides by a largest or mean magnitude, that divisor is 1e-20 or more.
Results may differ from a plain program's by a relative error of at most 0.009.
Values may be sent and summed in bfloat16 or wider, within the bound.
A program may use at most 32 MiB of HBM per device.

v0:
```python
import jax
import jax.numpy as jnp
from jax import lax
from jax.sharding import PartitionSpec as P


def body(tokens, gate_act, up_act, down_weight, norm_gain):
    hidden = (jax.nn.silu(gate_act.astype(jnp.float32)) * up_act.astype(jnp.float32)).astype(
        jnp.bfloat16
    )
    product = jnp.dot(hidden, down_weight, preferred_element_type=jnp.float32)
    summed = lax.psum_scatter(
        product.astype(jnp.bfloat16), "tensor", scatter_dimension=0, tiled=True
    ).astype(jnp.float32)
    residual = tokens.astype(jnp.float32) + summed
    mean_square = jnp.mean(residual * residual, axis=1, keepdims=True)
    normed = residual * lax.rsqrt(mean_square + 1e-05) * norm_gain[None, :]
    row_scale = jnp.max(jnp.abs(normed), axis=1)
    quantized = (normed / row_scale[:, None]).astype(jnp.bfloat16)
    all_rows, all_scales = (
        lax.all_gather(quantized, "tensor", axis=0, tiled=True),
        lax.all_gather(row_scale.astype(jnp.bfloat16), "tensor", axis=0, tiled=True).astype(
            row_scale.dtype
        ),
    )
    return (residual.astype(jnp.bfloat16), all_rows, all_scales)


def solution(mesh):
    return jax.shard_map(
        body,
        mesh=mesh,
        in_specs=(
            P(("dp", "tensor"), None),
            P("dp", "tensor"),
            P("dp", "tensor"),
            P("tensor", None),
            P(),
        ),
        out_specs=(P(("dp", "tensor"), None), P("dp", None), P("dp")),
        check_vma=False,
    )
```

profile of v0, /device:TPU:24, one launch (start us, length us, event | category | flops | bytes accessed | tf_op | source)
XLA Modules:
  0.0 219.6 jit_solution(5316129809443436352)
XLA Ops:
  7.2 0.0 copy-start
  7.2 0.0 copy-start.1
  7.2 0.0 reduce-scatter.2.cloned.1.call-start
  7.2 6.8 %convolution_convert_fusion = bf16[128,4096]{1,0:T(8,128)(2,1)} fusion(bf16[1280,4096]{1,0:T(8,128)(2,1)} %param.8, bf16[128,1280]{1,0:T(8,128)(2,1)} %param.7, bf16[128,1280]{1,0:T(8,128)(2,1)} %param.6), kind=kOutput, calls=%fused_computation | convolution fusion | flops 1344012288 | bytes 12189696 | tf_op jit(solution)/shard_map/dot_general | solution.py:11
  14.0 0.0 reduce-scatter.2.cloned.1.call-update
  14.0 0.0 all-gather.2.cloned.1.call-start
  14.1 116.5 %reduce-scatter.2.cloned.1.call-done = bf16[16,4096]{1,0:T(8,128)(2,1)} async-done(((bf16[128,4096]{1,0:T(8,128)(2,1)}), bf16[16,4096]{1,0:T(8,128)(2,1)}) %reduce-scatter.2.cloned.1.call-update) | async-done | bytes 131088 | tf_op jit(solution)/shard_map/reduce_scatter | solution.py:12
  130.6 0.0 copy-done
  130.6 1.1 multiply_reduce_fusion
  131.7 0.0 copy-done.1
  131.7 1.1 abs_reduce_fusion
  132.8 1.7 divide_convert_fusion
  134.5 0.0 all-gather.2.cloned.1.call-update
  134.5 1.3 dynamic-slice
  136.5 0.2 dynamic-update-slice
  136.7 29.9 %all-reduce = bf16[128]{0:T(256)(128)(2,1)S(1)} all-reduce(bf16[128]{0:T(256)(128)(2,1)S(1)} %dynamic-update-slice), channel_id=1, replica_groups=mesh['dp'=96,'tensor'=8] {'tensor'}, use_global_device_ids=true, to_apply=%add | all-reduce | flops 128 | bytes 512
  166.6 0.5 convert_element_type.39
  167.2 43.3 %all-gather.2.cloned.1.call-done = bf16[128,4096]{1,0:T(8,128)(2,1)} async-done(((bf16[16,4096]{1,0:T(8,128)(2,1)}), bf16[128,4096]{1,0:T(8,128)(2,1)}) %all-gather.2.cloned.1.call-update) | async-done | bytes 1048592 | tf_op jit(solution)/shard_map/all_gather | solution.py:21
  210.5 2.3 %copy.10 = bf16[128,4096]{1,0:T(8,128)(2,1)} copy(bf16[128,4096]{1,0:T(8,128)(2,1)} %all-gather.2.cloned.1.call-done) | data formatting | bytes 2097152
  (3 shorter events, 0.0 us)
Async XLA Ops:
  7.2 123.5 %copy-start = (bf16[16,4096]{1,0:T(8,128)(2,1)S(1)}, bf16[16,4096]{1,0:T(8,128)(2,1)}, u32[]{:S(2)}) copy-start(bf16[16,4096]{1,0:T(8,128)(2,1)} %param.5) | copy-start | bytes 393220
  7.2 124.5 %copy-start.1 = (f32[4096]{0:T(1024)S(1)}, f32[4096]{0:T(1024)}, u32[]{:S(2)}) copy-start(f32[4096]{0:T(1024)} %param.9) | copy-start | bytes 49156
  7.2 123.5 %reduce-scatter.2.cloned.1.call-start = ((), (), s32[]{:S(2)}) async-start(), calls=%async_computation.1 | async-start | bytes 1179648 | tf_op jit(solution)/shard_map/reduce_scatter | solution.py:12
  14.0 196.4 %all-gather.2.cloned.1.call-start = ((), (), s32[]{:S(2)}) async-start(), calls=%async_computation.2 | async-start | bytes 1179648 | tf_op jit(solution)/shard_map/all_gather | solution.py:21
Sparse Core Ops, SparseCore 0:
  14.2 116.4 reduce-scatter.1
  135.0 75.4 all-gather.1
where the time goes:
time: 220 us
  waiting for transfers between devices  160 us (73%)
  blocking collectives  29.9 us (14%)
  between operations  14.7 us (7%)
  matrix products  6.79 us (3%)
  other arithmetic  4.37 us (2%)
  local copies, waits for them, and re-layouts  3.82 us (2%)
    reduce_scatter x1, waiting for transfers between devices, body(): lax.psum_scatter(product.astype(jnp.bfloat16), 'tensor', scatter_dimensio...  117 us
    all_gather x1, waiting for transfers between devices, body(): lax.all_gather(quantized, 'tensor', axis=0, tiled=True)  43.3 us
    unnamed x1, blocking collectives  29.9 us
    dot_general x1, matrix products, body(): product = jnp.dot(hidden, down_weight, preferred_element_type=jnp.float32)  6.79 us
  transfers between devices with their start and end apart: 2, of which 2 were waited for; matrix products, arithmetic and copies ran while one was open for 1% of the time, Pallas kernels for 0%

commit v1 on v0

v1 whole, which is shorter than its diff:
```python
import functools

import jax
import jax.numpy as jnp
from jax import lax
from jax.experimental import pallas as pl
from jax.experimental.pallas import tpu as pltpu
from jax.sharding import PartitionSpec as P

MESH = pl.DeviceIdType.MESH
N_X = 4
N_Z = 2
WIDTH = 512
EARLY = 3
LAG = 2
LANES = 128


def exchange(
    tokens, gate, up, weight, gain,
    rows, square, peak,
    gate_v, up_v, weight_v, tokens_v, hidden, product, parts, partial, other,
    load, rs_send, rs_recv, z_send, z_recv, ag_send, ag_recv,
):
    n = product.shape[0]
    block = parts.shape[2]
    own = tokens_v.shape[0]
    me = lax.axis_index("tensor")
    x, z = me // N_Z, me % N_Z

    def along_x(d):
        return {"tensor": ((x + d) % N_X) * N_Z + z}

    along_z = {"tensor": x * N_Z + (1 - z)}

    barrier = pltpu.get_barrier_semaphore()
    for d in range(1, N_X):
        pl.semaphore_signal(barrier, inc=1, device_id=along_x(d), device_id_type=MESH)
    pl.semaphore_signal(barrier, inc=1, device_id=along_z, device_id_type=MESH)

    def weight_copy(c):
        columns = pl.ds(pl.multiple_of(c * WIDTH, WIDTH), WIDTH)
        return pltpu.make_async_copy(weight.at[:, columns], weight_v.at[c], load.at[3 + c])

    gate_copy = pltpu.make_async_copy(gate, gate_v, load.at[0])
    up_copy = pltpu.make_async_copy(up, up_v, load.at[1])
    tokens_copy = pltpu.make_async_copy(tokens, tokens_v, load.at[2])
    gate_copy.start()
    up_copy.start()
    for c in range(n):
        weight_copy(c).start()
    tokens_copy.start()

    gate_copy.wait()
    up_copy.wait()
    g = gate_v[...].astype(jnp.float32)
    hidden[...] = (g / (1.0 + jnp.exp(-g)) * up_v[...].astype(jnp.float32)).astype(hidden.dtype)

    def multiply(c):
        weight_copy(c).wait()
        product[c] = jnp.dot(
            hidden[...], weight_v[c], preferred_element_type=jnp.float32
        ).astype(product.dtype)

    def block_rows(i):
        return pl.ds(pl.multiple_of(i * block, block), block)

    def rs_copy(c, d):
        return pltpu.make_async_remote_copy(
            src_ref=product.at[c, block_rows((x + d) % N_X)],
            dst_ref=parts.at[c, d - 1],
            send_sem=rs_send.at[c, d - 1],
            recv_sem=rs_recv.at[c, d - 1],
            device_id=along_x(d),
            device_id_type=MESH,
        )

    def z_copy(c):
        return pltpu.make_async_remote_copy(
            src_ref=partial.at[c],
            dst_ref=other.at[c],
            send_sem=z_send.at[c],
            recv_sem=z_recv.at[c],
            device_id=along_z,
            device_id_type=MESH,
        )

    def ag_copy(c, d):
        return pltpu.make_async_remote_copy(
            src_ref=rows.at[c, block_rows(x)],
            dst_ref=rows.at[c, block_rows(x)],
            send_sem=ag_send.at[c, d - 1],
            recv_sem=ag_recv.at[c, d - 1],
            device_id=along_x(d),
            device_id_type=MESH,
        )

    def ag_arrival(c, d):
        return pltpu.make_async_remote_copy(
            src_ref=rows.at[c, block_rows((x + N_X - d) % N_X)],
            dst_ref=rows.at[c, block_rows((x + N_X - d) % N_X)],
            send_sem=ag_send.at[c, d - 1],
            recv_sem=ag_recv.at[c, d - 1],
            device_id=along_x(d),
            device_id_type=MESH,
        )

    def scatter(c):
        for d in (2, 1, 3):
            rs_copy(c, d).start()

    @pl.loop(0, EARLY)
    def _(c):
        multiply(c)

    pl.semaphore_wait(barrier, N_X)

    @pl.loop(0, EARLY)
    def _(c):
        scatter(c)

    @pl.loop(EARLY, n)
    def _(c):
        multiply(c)
        scatter(c)

    tokens_copy.wait()

    @pl.loop(0, n)
    def _(c):
        for d in range(1, N_X):
            rs_copy(c, d).wait_recv()
        total = product[c, block_rows(x)].astype(jnp.float32)
        for d in range(N_X - 1):
            total += parts[c, d].astype(jnp.float32)
        partial[c] = total.astype(partial.dtype)
        mine = pl.ds(pl.multiple_of(z * own, own), own)
        first = product[c, pl.ds(pl.multiple_of(x * block + z * own, own), own)].astype(jnp.float32)
        for d in range(N_X - 1):
            first += parts[c, d, mine].astype(jnp.float32)
        columns = pl.ds(pl.multiple_of(c * WIDTH, WIDTH), WIDTH)
        first += tokens_v[:, columns].astype(jnp.float32)
        partial[c, mine] = first.astype(partial.dtype)
        z_copy(c).start()

    square[...] = jnp.zeros_like(square)
    peak[...] = jnp.zeros_like(peak)

    def statistics(c):
        for d in range(1, N_X):
            ag_arrival(c, d).wait_recv()
        s, p = square[...], peak[...]
        for k in range(WIDTH // LANES):
            r = rows[c, :, k * LANES : (k + 1) * LANES].astype(jnp.float32)
            weight_of = gain[:, pl.ds(pl.multiple_of(c * WIDTH + k * LANES, LANES), LANES)]
            s += r * r
            p = jnp.maximum(p, jnp.abs(r * weight_of))
        square[...] = s
        peak[...] = p

    @pl.loop(0, n)
    def _(c):
        z_copy(c).wait_recv()
        rows[c, block_rows(x)] = (
            partial[c].astype(jnp.float32) + other[c].astype(jnp.float32)
        ).astype(rows.dtype)
        for d in (2, 1, 3):
            ag_copy(c, d).start()

        @pl.when(c >= LAG)
        def _():
            statistics(c - LAG)

    @pl.loop(n - LAG, n)
    def _(c):
        statistics(c)

    @pl.loop(0, n)
    def _(c):
        for d in range(1, N_X):
            rs_copy(c, d).wait_send()
            ag_copy(c, d).wait_send()
        z_copy(c).wait_send()


def scale(rows, square, peak, gain, residual_out, next_rows, next_scale, staged, sem):
    n, tokens, _ = rows.shape
    own = residual_out.shape[0]
    me = lax.axis_index("tensor")
    mine = pl.ds(pl.multiple_of(me * own, own), own)
    columns = [slice(c * WIDTH, (c + 1) * WIDTH) for c in range(n)]
    for c in range(n):
        residual_out[:, columns[c]] = rows[c, mine]
    blocks = 4
    size = tokens // blocks
    copies = []
    for b in range(blocks):
        these = slice(b * size, (b + 1) * size)
        inverse = 1.0 / jnp.max(peak[these], axis=1, keepdims=True)
        for c in range(n):
            r = rows[c, these].astype(jnp.float32)
            staged[these, columns[c]] = (r * gain[:, columns[c]] * inverse).astype(staged.dtype)
        copies.append(pltpu.make_async_copy(staged.at[these], next_rows.at[these], sem.at[b]))
        copies[-1].start()
    features = n * WIDTH
    mean = jnp.sum(square[...].T, axis=0, keepdims=True) * (1.0 / features)
    next_scale[...] = jnp.max(peak[...].T, axis=0, keepdims=True) * lax.rsqrt(mean + 1e-05)
    for copy in copies:
        copy.wait()


def body(tokens, gate, up, weight, gain):
    own, features = tokens.shape
    count, hidden_units = gate.shape
    n = features // WIDTH
    block = own * N_Z
    gain = gain.reshape(1, features)
    tokens, gate, up, weight = (pltpu.with_memory_space_constraint(a, pltpu.HBM) for a in (tokens, gate, up, weight))
    vmem, hbm = pl.BlockSpec(memory_space=pltpu.VMEM), pl.BlockSpec(memory_space=pltpu.HBM)
    bf16, f32 = jnp.bfloat16, jnp.float32
    dma = pltpu.SemaphoreType.DMA
    rows, square, peak = pl.pallas_call(
        exchange,
        out_shape=(
            jax.ShapeDtypeStruct((n, count, WIDTH), bf16),
            jax.ShapeDtypeStruct((count, LANES), f32),
            jax.ShapeDtypeStruct((count, LANES), f32),
        ),
        in_specs=[hbm, hbm, hbm, hbm, vmem],
        out_specs=(vmem, vmem, vmem),
        scratch_shapes=[
            pltpu.VMEM((count, hidden_units), bf16),
            pltpu.VMEM((count, hidden_units), bf16),
            pltpu.VMEM((n, hidden_units, WIDTH), bf16),
            pltpu.VMEM((own, features), bf16),
            pltpu.VMEM((count, hidden_units), bf16),
            pltpu.VMEM((n, count, WIDTH), bf16),
            pltpu.VMEM((n, N_X - 1, block, WIDTH), bf16),
            pltpu.VMEM((n, block, WIDTH), bf16),
            pltpu.VMEM((n, block, WIDTH), bf16),
            dma((3 + n,)),
            dma((n, N_X - 1)),
            dma((n, N_X - 1)),
            dma((n,)),
            dma((n,)),
            dma((n, N_X - 1)),
            dma((n, N_X - 1)),
        ],
        compiler_params=pltpu.CompilerParams(collective_id=0, has_side_effects=True, vmem_limit_bytes=52_000_000),
        name="exchange",
    )(tokens, gate, up, weight, gain)
    residual_out, next_rows, next_scale = pl.pallas_call(
        scale,
        out_shape=(
            jax.ShapeDtypeStruct((own, features), bf16),
            jax.ShapeDtypeStruct((count, features), bf16),
            jax.ShapeDtypeStruct((1, count), f32),
        ),
        in_specs=[vmem, vmem, vmem, vmem],
        out_specs=(vmem, hbm, vmem),
        scratch_shapes=[pltpu.VMEM((count, features), bf16), dma((4,))],
        compiler_params=pltpu.CompilerParams(vmem_limit_bytes=8 << 20),
        name="scale",
    )(rows, square, peak, gain)
    return residual_out, next_rows, next_scale.reshape(count)


def solution(mesh):
    return jax.shard_map(
        body,
        mesh=mesh,
        in_specs=(
            P(("dp", "tensor"), None),
            P("dp", "tensor"),
            P("dp", "tensor"),
            P("tensor", None),
            P(),
        ),
        out_specs=(P(("dp", "tensor"), None), P("dp", None), P("dp")),
        check_vma=False,
    )
```

time: 220 us -> 46.6 us (0.21)
  the two profiles are of different devices: /device:TPU:24 before, /device:TPU:264 now
where the time goes in v1:
time: 46.6 us; the launch traced here: 46.4 us
  Pallas kernels  45.1 us (97%)
  local copies, waits for them, and re-layouts  0.71 us (2%)
  between operations  0.65 us (1%)
    pallas_call x1, Pallas kernels, body(): pl.pallas_call(exchange, out_shape=(jax.ShapeDtypeStruct((n, count, WIDTH...  43.3 us
    pallas_call x1, Pallas kernels, body(): pl.pallas_call(scale, out_shape=(jax.ShapeDtypeStruct((own, features), bf...  1.77 us

profile of v1, /device:TPU:264, one launch (start us, length us, event | category | flops | bytes accessed | tf_op | source)
XLA Modules:
  0.0 46.4 jit_solution(14535817503069623007)
XLA Ops:
  0.6 0.0 copy-start
  0.6 0.7 %copy-done = f32[4096]{0:T(1024)S(1)} copy-done((f32[4096]{0:T(1024)S(1)}, f32[4096]{0:T(1024)}, u32[]{:S(2)}) %copy-start) | copy-done | bytes 16408
  1.4 43.3 %exchange.1 = (bf16[8,128,512]{2,1,0:T(8,128)(2,1)S(1)}, f32[128,128]{1,0:T(8,128)S(1)}, f32[128,128]{1,0:T(8,128)S(1)}) custom-call(bf16[16,4096]{1,0:T(8,128)(2,1)} %tokens.1, bf16[128,1280]{1,0:T(8,128)(2,1)} %gate.1, bf16[128,1280]{1,0:T(8,128)(2,1)} %up.1, bf16[1280,4096]{1,0:T(8,128)(2,1)} %weight.1, f32[1,4096]{1,0:T(1,128)S(1)} %bitcast.2), custom_call_target="tpu_custom_call" | custom-call | tf_op jit(solution)/shard_map/exchange/pallas_call | solution.py:222
  44.7 1.8 %scale.1 = (bf16[16,4096]{1,0:T(8,128)(2,1)}, bf16[128,4096]{1,0:T(8,128)(2,1)}, f32[1,128]{1,0:T(1,128)}) custom-call(bf16[8,128,512]{2,1,0:T(8,128)(2,1)S(1)} %get-tuple-element.9.rows, f32[128,128]{1,0:T(8,128)S(1)} %get-tuple-element.10.square, f32[128,128]{1,0:T(8,128)S(1)} %get-tuple-element.11.peak, f32[1,4096]{1,0:T(1,128)S(1)} %bitcast.3), custom_call_target="tpu_custom_call" | custom-call | tf_op jit(solution)/shard_map/scale/pallas_call | solution.py:252
Async XLA Ops:
  0.6 0.7 %copy-start = (f32[4096]{0:T(1024)S(1)}, f32[4096]{0:T(1024)}, u32[]{:S(2)}) copy-start(f32[4096]{0:T(1024)} %param.9) | copy-start | bytes 49156

commit v2 on v1

v2 whole, which is shorter than its diff:
```python
import contextlib

import jax
import jax.numpy as jnp
from jax import lax
from jax.experimental import pallas as pl
from jax.experimental.pallas import tpu as pltpu
from jax.sharding import PartitionSpec as P

MESH = pl.DeviceIdType.MESH
N_X = 4
N_Z = 2
N_LO = 6
N_CORES = 2
WIDTH = 256
SPAN = 2
LAG = 4
LANES = 128
BLOCKS = 8
PACE = 3
AHEAD = 8


def scope(name):
    return contextlib.nullcontext()


def exchange(
    tokens, gate, up, weight, gain_in,
    rows, square, peak, gain,
    acts, weight_v, tokens_v, hidden, product, parts, partial, other,
    load, ready, rs_send, rs_recv, z_send, z_recv, ag_send, ag_recv,
):
    n = product.shape[0]
    block = parts.shape[2]
    own = tokens_v.shape[0]
    me = lax.axis_index("tensor")
    x, z = me // N_Z, me % N_Z

    turn = (lax.axis_index("dp") // N_CORES) % N_LO // 2

    def along_x(d):
        return {"tensor": ((x + d) % N_X) * N_Z + z}

    along_z = {"tensor": x * N_Z + (1 - z)}

    barrier = pltpu.get_barrier_semaphore()
    for d in range(1, N_X):
        pl.semaphore_signal(barrier, inc=1, device_id=along_x(d), device_id_type=MESH)

    @pl.when(z == 0)
    def _():
        pl.semaphore_signal(barrier, inc=1, device_id=along_z, device_id_type=MESH)

    def weight_copy(b):
        columns = pl.ds(pl.multiple_of(b * SPAN * WIDTH, WIDTH), SPAN * WIDTH)
        return pltpu.make_async_copy(weight.at[:, columns], weight_v.at[b], load.at[3 + b])

    gate_copy = pltpu.make_async_copy(gate, acts.at[0], load.at[0])
    up_copy = pltpu.make_async_copy(up, acts.at[1], load.at[0])
    tokens_copy = pltpu.make_async_copy(tokens, tokens_v, load.at[1])
    gain_copy = pltpu.make_async_copy(gain_in, gain, load.at[2])
    gate_copy.start()
    up_copy.start()
    weight_copy(0).start()
    with scope("load_wait"):
        pltpu.make_async_copy(acts, acts, load.at[0]).wait()
    for b in range(1, n // SPAN):
        weight_copy(b).start()
    tokens_copy.start()
    gain_copy.start()
    g = acts[0].astype(jnp.float32)
    hidden[...] = (g / (1.0 + jnp.exp(-g)) * acts[1].astype(jnp.float32)).astype(hidden.dtype)

    def multiply(b):
        weight_copy(b).wait()
        result = jnp.dot(hidden[...], weight_v[b], preferred_element_type=jnp.float32)
        for k in range(SPAN):
            product[b * SPAN + k] = result[:, k * WIDTH : (k + 1) * WIDTH].astype(product.dtype)

    def block_rows(i):
        return pl.ds(pl.multiple_of(i * block, block), block)

    def rs_copy(c, d):
        return pltpu.make_async_remote_copy(
            src_ref=product.at[c, block_rows((x + d) % N_X)],
            dst_ref=parts.at[c, d - 1],
            send_sem=rs_send,
            recv_sem=rs_recv.at[c],
            device_id=along_x(d),
            device_id_type=MESH,
        )

    def z_copy(c):
        return pltpu.make_async_remote_copy(
            src_ref=partial.at[c],
            dst_ref=other.at[c],
            send_sem=z_send,
            recv_sem=z_recv.at[c],
            device_id=along_z,
            device_id_type=MESH,
        )

    def z_copies(first, end):
        @pl.loop(first, end)
        def _(c):
            z_copy(c).start()

    def ag_copy(c, d):
        return pltpu.make_async_remote_copy(
            src_ref=rows.at[c, block_rows(x)],
            dst_ref=rows.at[c, block_rows(x)],
            send_sem=ag_send,
            recv_sem=ag_recv.at[c],
            device_id=along_x(d),
            device_id_type=MESH,
        )

    def arrived(of_three, sem):
        pltpu.make_async_copy(of_three, of_three, sem).wait()

    def scatter(c):
        for d in (2, 1, 3):
            rs_copy(c, d).start()

    with scope("barrier_w"):
        pl.semaphore_wait(barrier, N_X - 1 + z)

    @pl.when(z == 1)
    def _():
        pl.semaphore_signal(ready, inc=1, device_id=along_z, device_id_type=MESH)

    @pl.loop(0, n // SPAN)
    def _(b):
        with scope("mm"):
            multiply(b)
        for k in range(SPAN):
            scatter(b * SPAN + k)

    tokens_copy.wait()
    gain_copy.wait()

    @pl.loop(0, n)
    def _(c):
        with scope("rs_wait"):
            arrived(parts.at[c], rs_recv.at[c])
        total = product[c, block_rows(x)].astype(jnp.float32)
        for d in range(N_X - 1):
            total += parts[c, d].astype(jnp.float32)
        partial[c] = total.astype(partial.dtype)
        mine = pl.ds(pl.multiple_of(z * own, own), own)
        first = product[c, pl.ds(pl.multiple_of(x * block + z * own, own), own)].astype(jnp.float32)
        for d in range(N_X - 1):
            first += parts[c, d, mine].astype(jnp.float32)
        columns = pl.ds(pl.multiple_of(c * WIDTH, WIDTH), WIDTH)
        first += tokens_v[:, columns].astype(jnp.float32)
        partial[c, mine] = first.astype(partial.dtype)

        sent = (c * (PACE - turn) + PACE - 1) // PACE
        due = jnp.where(c == n - 1, n, ((c + 1) * (PACE - turn) + PACE - 1) // PACE)

        @pl.when(z == 1)
        def _():
            z_copies(sent, due)

    ahead = AHEAD + turn // 2

    @pl.when(z == 0)
    def _():
        with scope("ready_w"):
            pl.semaphore_wait(ready, 1)
        z_copies(0, ahead)

    square[...] = jnp.zeros_like(square)
    peak[...] = jnp.zeros_like(peak)

    def statistics(c):
        with scope("ag_wait"):
            arrived(parts.at[c], ag_recv.at[c])
        s, p = square[...], peak[...]
        for k in range(WIDTH // LANES):
            r = rows[c, :, k * LANES : (k + 1) * LANES].astype(jnp.float32)
            weight_of = gain[:, pl.ds(pl.multiple_of(c * WIDTH + k * LANES, LANES), LANES)]
            s += r * r
            p = jnp.maximum(p, jnp.abs(r * weight_of))
        square[...] = s
        peak[...] = p

    @pl.loop(0, n)
    def _(c):
        with scope("z_wait"):
            z_copy(c).wait_recv()
        rows[c, block_rows(x)] = (
            partial[c].astype(jnp.float32) + other[c].astype(jnp.float32)
        ).astype(rows.dtype)
        for d in (2, 1, 3):
            ag_copy(c, d).start()

        @pl.when((z == 0) & (c > 0) & (c + ahead <= n))
        def _():
            z_copy(c + ahead - 1).start()

        @pl.when(c >= LAG)
        def _():
            statistics(c - LAG)

    @pl.loop(n - LAG, n)
    def _(c):
        statistics(c)

    with scope("send_wait"):
        arrived(parts, rs_send)
        arrived(parts, ag_send)
        arrived(partial, z_send)


def scale(rows, square, peak, gain, residual_out, next_rows, next_scale, kept, staged, scales, sem):
    n, tokens, _ = rows.shape
    own = kept.shape[0]
    me = lax.axis_index("tensor")
    mine = pl.ds(pl.multiple_of(me * own, own), own)
    columns = [slice(c * WIDTH, (c + 1) * WIDTH) for c in range(n)]
    for c in range(n):
        kept[:, columns[c]] = rows[c, mine]
    size = tokens // BLOCKS
    copies = [pltpu.make_async_copy(kept, residual_out, sem.at[BLOCKS])]
    copies[-1].start()
    mean = jnp.sum(square[...].T, axis=0, keepdims=True) * (1.0 / (n * WIDTH))
    scales[...] = jnp.max(peak[...].T, axis=0, keepdims=True) * lax.rsqrt(mean + 1e-05)
    copies.append(pltpu.make_async_copy(scales, next_scale, sem.at[BLOCKS + 1]))
    copies[-1].start()
    for b in range(BLOCKS):
        these = slice(b * size, (b + 1) * size)
        inverse = 1.0 / jnp.max(peak[these], axis=1, keepdims=True)
        for c in range(n):
            r = rows[c, these].astype(jnp.float32)
            staged[these, columns[c]] = (r * gain[:, columns[c]] * inverse).astype(staged.dtype)
        copies.append(pltpu.make_async_copy(staged.at[these], next_rows.at[these], sem.at[b]))
        copies[-1].start()
    for copy in copies:
        copy.wait()


def body(tokens, gate, up, weight, gain):
    own, features = tokens.shape
    count, hidden_units = gate.shape
    n = features // WIDTH
    block = own * N_Z
    gain = gain.reshape(1, features)
    tokens, gate, up, weight, gain = (pltpu.with_memory_space_constraint(a, pltpu.HBM) for a in (tokens, gate, up, weight, gain))
    vmem, hbm = pl.BlockSpec(memory_space=pltpu.VMEM), pl.BlockSpec(memory_space=pltpu.HBM)
    bf16, f32 = jnp.bfloat16, jnp.float32
    dma = pltpu.SemaphoreType.DMA
    rows, square, peak, gain = pl.pallas_call(
        exchange,
        out_shape=(
            jax.ShapeDtypeStruct((n, count, WIDTH), bf16),
            jax.ShapeDtypeStruct((count, LANES), f32),
            jax.ShapeDtypeStruct((count, LANES), f32),
            jax.ShapeDtypeStruct((1, features), f32),
        ),
        in_specs=[hbm] * 5,
        out_specs=(vmem,) * 4,
        scratch_shapes=[
            pltpu.VMEM((2, count, hidden_units), bf16),
            pltpu.VMEM((n // SPAN, hidden_units, SPAN * WIDTH), bf16),
            pltpu.VMEM((own, features), bf16),
            pltpu.VMEM((count, hidden_units), bf16),
            pltpu.VMEM((n, count, WIDTH), bf16),
            pltpu.VMEM((n, N_X - 1, block, WIDTH), bf16),
            pltpu.VMEM((n, block, WIDTH), bf16),
            pltpu.VMEM((n, block, WIDTH), bf16),
            dma((3 + n // SPAN,)),
            pltpu.SemaphoreType.REGULAR,
            dma,
            dma((n,)),
            dma,
            dma((n,)),
            dma,
            dma((n,)),
        ],
        compiler_params=pltpu.CompilerParams(collective_id=0, has_side_effects=True, vmem_limit_bytes=52_000_000),
        name="exchange",
    )(tokens, gate, up, weight, gain)
    residual_out, next_rows, next_scale = pl.pallas_call(
        scale,
        out_shape=(
            jax.ShapeDtypeStruct((own, features), bf16),
            jax.ShapeDtypeStruct((count, features), bf16),
            jax.ShapeDtypeStruct((1, count), f32),
        ),
        in_specs=[vmem] * 4,
        out_specs=(hbm,) * 3,
        scratch_shapes=[
            pltpu.VMEM((own, features), bf16),
            pltpu.VMEM((count, features), bf16),
            pltpu.VMEM((1, count), f32),
            dma((BLOCKS + 2,)),
        ],
        compiler_params=pltpu.CompilerParams(vmem_limit_bytes=8 << 20),
        name="scale",
    )(rows, square, peak, gain)
    return residual_out, next_rows, next_scale.reshape(count)


def solution(mesh):
    return jax.shard_map(
        body,
        mesh=mesh,
        in_specs=(
            P(("dp", "tensor"), None),
            P("dp", "tensor"),
            P("dp", "tensor"),
            P("tensor", None),
            P(),
        ),
        out_specs=(P(("dp", "tensor"), None), P("dp", None), P("dp")),
        check_vma=False,
    )
```

time: 46.6 us -> 45.5 us (0.976)
  the two profiles are of different devices: /device:TPU:264 before, /device:TPU:256 now
where the time goes in v2:
time: 45.5 us; the launch traced here: 45.3 us
  Pallas kernels  44.7 us (98%)
  between operations  0.64 us (1%)
    pallas_call x1, Pallas kernels, body(): pl.pallas_call(exchange, out_shape=(jax.ShapeDtypeStruct((n, count, WIDTH...  43.5 us
    pallas_call x1, Pallas kernels, body(): pl.pallas_call(scale, out_shape=(jax.ShapeDtypeStruct((own, features), bf...  1.2 us

profile of v2, /device:TPU:256, one launch (start us, length us, event | category | flops | bytes accessed | tf_op | source)
XLA Modules:
  0.0 45.3 jit_solution(3905521870437291662)
XLA Ops:
  0.6 43.5 %exchange.1 = (bf16[16,128,256]{2,1,0:T(8,128)(2,1)S(1)}, f32[128,128]{1,0:T(8,128)S(1)}, f32[128,128]{1,0:T(8,128)S(1)}, f32[1,4096]{1,0:T(1,128)S(1)}) custom-call(bf16[16,4096]{1,0:T(8,128)(2,1)} %tokens.1, bf16[128,1280]{1,0:T(8,128)(2,1)} %gate.1, bf16[128,1280]{1,0:T(8,128)(2,1)} %up.1, bf16[1280,4096]{1,0:T(8,128)(2,1)} %weight.1, f32[1,4096]{1,0:T(1,128)} %bitcast.2), custom_call_target="tpu_custom_call" | custom-call | tf_op jit(solution)/shard_map/exchange/pallas_call | solution.py:254
  44.2 1.2 %scale.1 = (bf16[16,4096]{1,0:T(8,128)(2,1)}, bf16[128,4096]{1,0:T(8,128)(2,1)}, f32[1,128]{1,0:T(1,128)}) custom-call(bf16[16,128,256]{2,1,0:T(8,128)(2,1)S(1)} %get-tuple-element.10.rows, f32[128,128]{1,0:T(8,128)S(1)} %get-tuple-element.11.square, f32[128,128]{1,0:T(8,128)S(1)} %get-tuple-element.12.peak, f32[1,4096]{1,0:T(1,128)S(1)} %get-tuple-element.13.gain), custom_call_target="tpu_custom_call" | custom-call | tf_op jit(solution)/shard_map/scale/pallas_call | solution.py:285

commit v3 on v2

--- a/solution.py
+++ b/solution.py
@@ -14,11 +14,11 @@
 N_CORES = 2
 WIDTH = 256
 SPAN = 2
-LAG = 4
+LAG = 12
 LANES = 128
 BLOCKS = 8
-PACE = 3
-AHEAD = 8
+PACE = 6
+AHEAD = 4
 
 
 def scope(name):
@@ -37,7 +37,9 @@
     me = lax.axis_index("tensor")
     x, z = me // N_Z, me % N_Z
 
-    turn = (lax.axis_index("dp") // N_CORES) % N_LO // 2
+    core, low = lax.axis_index("dp") % N_CORES, (lax.axis_index("dp") // N_CORES) % N_LO
+    turn, odd = low // 2, low % 2
+    pace = jnp.where(turn == 0, PACE, jnp.where(turn == 1, 4 + odd, PACE - 3 * odd))
 
     def along_x(d):
         return {"tensor": ((x + d) % N_X) * N_Z + z}
@@ -63,12 +65,12 @@
     gate_copy.start()
     up_copy.start()
     weight_copy(0).start()
-    with scope("load_wait"):
-        pltpu.make_async_copy(acts, acts, load.at[0]).wait()
     for b in range(1, n // SPAN):
         weight_copy(b).start()
     tokens_copy.start()
     gain_copy.start()
+    with scope("load_wait"):
+        pltpu.make_async_copy(acts, acts, load.at[0]).wait()
     g = acts[0].astype(jnp.float32)
     hidden[...] = (g / (1.0 + jnp.exp(-g)) * acts[1].astype(jnp.float32)).astype(hidden.dtype)
 
@@ -123,6 +125,8 @@
         for d in (2, 1, 3):
             rs_copy(c, d).start()
 
+    with scope("mm"):
+        multiply(0)
     with scope("barrier_w"):
         pl.semaphore_wait(barrier, N_X - 1 + z)
 
@@ -130,7 +134,10 @@
     def _():
         pl.semaphore_signal(ready, inc=1, device_id=along_z, device_id_type=MESH)
 
-    @pl.loop(0, n // SPAN)
+    for k in range(SPAN):
+        scatter(k)
+
+    @pl.loop(1, n // SPAN)
     def _(b):
         with scope("mm"):
             multiply(b)
@@ -156,14 +163,14 @@
         first += tokens_v[:, columns].astype(jnp.float32)
         partial[c, mine] = first.astype(partial.dtype)
 
-        sent = (c * (PACE - turn) + PACE - 1) // PACE
-        due = jnp.where(c == n - 1, n, ((c + 1) * (PACE - turn) + PACE - 1) // PACE)
+        sent = (c * pace + PACE - 1) // PACE
+        due = jnp.where(c == n - 1, n, ((c + 1) * pace + PACE - 1) // PACE)
 
         @pl.when(z == 1)
         def _():
             z_copies(sent, due)
 
-    ahead = AHEAD + turn // 2
+    ahead = AHEAD + 1 - 2 * core
 
     @pl.when(z == 0)
     def _():

time: 45.5 us -> 41.2 us (0.905)
  the two profiles are of different devices: /device:TPU:256 before, /device:TPU:176 now
where the time goes in v3:
time: 41.2 us; the launch traced here: 41 us
  Pallas kernels  40.4 us (98%)
  between operations  0.64 us (2%)
    pallas_call x1, Pallas kernels, body(): pl.pallas_call(exchange, out_shape=(jax.ShapeDtypeStruct((n, count, WIDTH...  39.2 us
    pallas_call x1, Pallas kernels, body(): pl.pallas_call(scale, out_shape=(jax.ShapeDtypeStruct((own, features), bf...  1.2 us

profile of v3, /device:TPU:176, one launch (start us, length us, event | category | flops | bytes accessed | tf_op | source)
XLA Modules:
  0.0 41.0 jit_solution(12452515430232153881)
XLA Ops:
  0.6 39.2 %exchange.1 = (bf16[16,128,256]{2,1,0:T(8,128)(2,1)S(1)}, f32[128,128]{1,0:T(8,128)S(1)}, f32[128,128]{1,0:T(8,128)S(1)}, f32[1,4096]{1,0:T(1,128)S(1)}) custom-call(bf16[16,4096]{1,0:T(8,128)(2,1)} %tokens.1, bf16[128,1280]{1,0:T(8,128)(2,1)} %gate.1, bf16[128,1280]{1,0:T(8,128)(2,1)} %up.1, bf16[1280,4096]{1,0:T(8,128)(2,1)} %weight.1, f32[1,4096]{1,0:T(1,128)} %bitcast.2), custom_call_target="tpu_custom_call" | custom-call | tf_op jit(solution)/shard_map/exchange/pallas_call | solution.py:261
  39.8 1.2 %scale.1 = (bf16[16,4096]{1,0:T(8,128)(2,1)}, bf16[128,4096]{1,0:T(8,128)(2,1)}, f32[1,128]{1,0:T(1,128)}) custom-call(bf16[16,128,256]{2,1,0:T(8,128)(2,1)S(1)} %get-tuple-element.10.rows, f32[128,128]{1,0:T(8,128)S(1)} %get-tuple-element.11.square, f32[128,128]{1,0:T(8,128)S(1)} %get-tuple-element.12.peak, f32[1,4096]{1,0:T(1,128)S(1)} %get-tuple-element.13.gain), custom_call_target="tpu_custom_call" | custom-call | tf_op jit(solution)/shard_map/scale/pallas_call | solution.py:292

commit v4 on v3

--- a/solution.py
+++ b/solution.py
@@ -16,7 +16,7 @@
 SPAN = 2
 LAG = 12
 LANES = 128
-BLOCKS = 8
+BLOCKS = 16
 PACE = 6
 AHEAD = 4
 
@@ -58,13 +58,19 @@
         columns = pl.ds(pl.multiple_of(b * SPAN * WIDTH, WIDTH), SPAN * WIDTH)
         return pltpu.make_async_copy(weight.at[:, columns], weight_v.at[b], load.at[3 + b])
 
+    def first_copy(k):
+        columns = pl.ds(k * WIDTH, WIDTH)
+        place = load.at[3 if k == 0 else 2 + n // SPAN + k]
+        return pltpu.make_async_copy(weight.at[:, columns], weight_v.at[0, :, columns], place)
+
     gate_copy = pltpu.make_async_copy(gate, acts.at[0], load.at[0])
     up_copy = pltpu.make_async_copy(up, acts.at[1], load.at[0])
     tokens_copy = pltpu.make_async_copy(tokens, tokens_v, load.at[1])
     gain_copy = pltpu.make_async_copy(gain_in, gain, load.at[2])
     gate_copy.start()
     up_copy.start()
-    weight_copy(0).start()
+    for k in range(SPAN):
+        first_copy(k).start()
     for b in range(1, n // SPAN):
         weight_copy(b).start()
     tokens_copy.start()
@@ -73,6 +79,12 @@
         pltpu.make_async_copy(acts, acts, load.at[0]).wait()
     g = acts[0].astype(jnp.float32)
     hidden[...] = (g / (1.0 + jnp.exp(-g)) * acts[1].astype(jnp.float32)).astype(hidden.dtype)
+
+    def multiply_first(k):
+        first_copy(k).wait()
+        product[k] = jnp.dot(
+            hidden[...], weight_v[0, :, k * WIDTH : (k + 1) * WIDTH], preferred_element_type=jnp.float32
+        ).astype(product.dtype)
 
     def multiply(b):
         weight_copy(b).wait()
@@ -126,7 +138,7 @@
             rs_copy(c, d).start()
 
     with scope("mm"):
-        multiply(0)
+        multiply_first(0)
     with scope("barrier_w"):
         pl.semaphore_wait(barrier, N_X - 1 + z)
 
@@ -134,7 +146,9 @@
     def _():
         pl.semaphore_signal(ready, inc=1, device_id=along_z, device_id_type=MESH)
 
-    for k in range(SPAN):
+    scatter(0)
+    for k in range(1, SPAN):
+        multiply_first(k)
         scatter(k)
 
     @pl.loop(1, n // SPAN)
@@ -277,7 +291,7 @@
             pltpu.VMEM((n, N_X - 1, block, WIDTH), bf16),
             pltpu.VMEM((n, block, WIDTH), bf16),
             pltpu.VMEM((n, block, WIDTH), bf16),
-            dma((3 + n // SPAN,)),
+            dma((2 + n // SPAN + SPAN,)),
             pltpu.SemaphoreType.REGULAR,
             dma,
             dma((n,)),

time: 41.2 us -> 41 us (level)
  the two profiles are of different devices: /device:TPU:176 before, /device:TPU:128 now
where the time goes in v4:
time: 41 us; the launch traced here: 40.9 us
  Pallas kernels  40.3 us (98%)
  between operations  0.64 us (2%)
    pallas_call x1, Pallas kernels, body(): pl.pallas_call(exchange, out_shape=(jax.ShapeDtypeStruct((n, count, WIDTH...  39 us
    pallas_call x1, Pallas kernels, body(): pl.pallas_call(scale, out_shape=(jax.ShapeDtypeStruct((own, features), bf...  1.26 us

profile of v4, /device:TPU:128, one launch (start us, length us, event | category | flops | bytes accessed | tf_op | source)
XLA Modules:
  0.0 40.9 jit_solution(15208726626473494213)
XLA Ops:
  0.6 39.0 %exchange.1 = (bf16[16,128,256]{2,1,0:T(8,128)(2,1)S(1)}, f32[128,128]{1,0:T(8,128)S(1)}, f32[128,128]{1,0:T(8,128)S(1)}, f32[1,4096]{1,0:T(1,128)S(1)}) custom-call(bf16[16,4096]{1,0:T(8,128)(2,1)} %tokens.1, bf16[128,1280]{1,0:T(8,128)(2,1)} %gate.1, bf16[128,1280]{1,0:T(8,128)(2,1)} %up.1, bf16[1280,4096]{1,0:T(8,128)(2,1)} %weight.1, f32[1,4096]{1,0:T(1,128)} %bitcast.2), custom_call_target="tpu_custom_call" | custom-call | tf_op jit(solution)/shard_map/exchange/pallas_call | solution.py:275
  39.7 1.3 %scale.1 = (bf16[16,4096]{1,0:T(8,128)(2,1)}, bf16[128,4096]{1,0:T(8,128)(2,1)}, f32[1,128]{1,0:T(1,128)}) custom-call(bf16[16,128,256]{2,1,0:T(8,128)(2,1)S(1)} %get-tuple-element.10.rows, f32[128,128]{1,0:T(8,128)S(1)} %get-tuple-element.11.square, f32[128,128]{1,0:T(8,128)S(1)} %get-tuple-element.12.peak, f32[1,4096]{1,0:T(1,128)S(1)} %get-tuple-element.13.gain), custom_call_target="tpu_custom_call" | custom-call | tf_op jit(solution)/shard_map/scale/pallas_call | solution.py:306

commit v5 on v4

--- a/solution.py
+++ b/solution.py
@@ -125,7 +125,7 @@
             src_ref=rows.at[c, block_rows(x)],
             dst_ref=rows.at[c, block_rows(x)],
             send_sem=ag_send,
-            recv_sem=ag_recv.at[c],
+            recv_sem=ag_recv.at[jnp.maximum(c - LAG + 1, 0)],
             device_id=along_x(d),
             device_id_type=MESH,
         )
@@ -196,8 +196,6 @@
     peak[...] = jnp.zeros_like(peak)
 
     def statistics(c):
-        with scope("ag_wait"):
-            arrived(parts.at[c], ag_recv.at[c])
         s, p = square[...], peak[...]
         for k in range(WIDTH // LANES):
             r = rows[c, :, k * LANES : (k + 1) * LANES].astype(jnp.float32)
@@ -221,12 +219,17 @@
         def _():
             z_copy(c + ahead - 1).start()
 
-        @pl.when(c >= LAG)
-        def _():
-            statistics(c - LAG)
-
-    @pl.loop(n - LAG, n)
+    with scope("ag_wait"):
+        arrived(parts.at[pl.ds(0, LAG)], ag_recv.at[0])
+
+    @pl.loop(0, LAG)
     def _(c):
+        statistics(c)
+
+    @pl.loop(LAG, n)
+    def _(c):
+        with scope("ag_wait"):
+            arrived(parts.at[c], ag_recv.at[c - LAG + 1])
         statistics(c)
 
     with scope("send_wait"):
@@ -298,7 +301,7 @@
             dma,
             dma((n,)),
             dma,
-            dma((n,)),
+            dma((n - LAG + 1,)),
         ],
         compiler_params=pltpu.CompilerParams(collective_id=0, has_side_effects=True, vmem_limit_bytes=52_000_000),
         name="exchange",

time: 41 us -> 40.9 us (level)
  no operation moved by 1% of the time
where the time goes in v5:
time: 40.9 us; the launch traced here: 40.8 us
  Pallas kernels  40.2 us (98%)
  between operations  0.64 us (2%)
    pallas_call x1, Pallas kernels, body(): pl.pallas_call(exchange, out_shape=(jax.ShapeDtypeStruct((n, count, WIDTH...  38.9 us
    pallas_call x1, Pallas kernels, body(): pl.pallas_call(scale, out_shape=(jax.ShapeDtypeStruct((own, features), bf...  1.26 us

profile of v5, /device:TPU:128, one launch (start us, length us, event | category | flops | bytes accessed | tf_op | source)
XLA Modules:
  0.0 40.8 jit_solution(5718629281590271947)
XLA Ops:
  0.6 38.9 %exchange.1 = (bf16[16,128,256]{2,1,0:T(8,128)(2,1)S(1)}, f32[128,128]{1,0:T(8,128)S(1)}, f32[128,128]{1,0:T(8,128)S(1)}, f32[1,4096]{1,0:T(1,128)S(1)}) custom-call(bf16[16,4096]{1,0:T(8,128)(2,1)} %tokens.1, bf16[128,1280]{1,0:T(8,128)(2,1)} %gate.1, bf16[128,1280]{1,0:T(8,128)(2,1)} %up.1, bf16[1280,4096]{1,0:T(8,128)(2,1)} %weight.1, f32[1,4096]{1,0:T(1,128)} %bitcast.2), custom_call_target="tpu_custom_call" | custom-call | tf_op jit(solution)/shard_map/exchange/pallas_call | solution.py:278
  39.6 1.3 %scale.1 = (bf16[16,4096]{1,0:T(8,128)(2,1)}, bf16[128,4096]{1,0:T(8,128)(2,1)}, f32[1,128]{1,0:T(1,128)}) custom-call(bf16[16,128,256]{2,1,0:T(8,128)(2,1)S(1)} %get-tuple-element.10.rows, f32[128,128]{1,0:T(8,128)S(1)} %get-tuple-element.11.square, f32[128,128]{1,0:T(8,128)S(1)} %get-tuple-element.12.peak, f32[1,4096]{1,0:T(1,128)S(1)} %get-tuple-element.13.gain), custom_call_target="tpu_custom_call" | custom-call | tf_op jit(solution)/shard_map/scale/pallas_call | solution.py:309
